TPU v7x, 256 devices: a whole 4x4x8 slice. The times are simulated.
256 devices in a mesh: user: 16 (over x, y_hi, core), item: 16 (over z, y_lo).
Axes of the slice: x: 4, y: 4 (y_hi: 2, y_lo: 2; y = y_hi * 2 + y_lo), z: 8, core: 2. Of those that a mesh axis runs over, the one named last changes fastest.
Arguments:
- item_factors: float32 [16, 4096, 128], P('item', 'user'), may hold values from -2 to 2
- weights: float32 [128, 256, 128, 128], P('user', 'item'), may hold values from 0 to 100
- tile_ids: int32 [128, 16, 16], P('user', 'item'), may hold values from 0 to 31, as said below
- start_factors: float32 [16384, 128], P('user'), may hold values from -4 to 4
Outputs:
- user_factors: float32 [16384, 128], P('user')
Inputs may be any that keep to these rules, and one draw needn't show every extreme that they name: `tile_ids`: entries of one user block and item block are distinct.
All inputs are finite; a program needn't handle non-finite values.
Results may differ from a plain program's by a relative error of at most 0.0003.
Values sent between devices are 32-bit elements; how exact they have to be, the bound alone decides.
A program may use at most 64 MiB of HBM per device.

v0:
```python
import jax
import jax.numpy as jnp
from jax import lax
from jax.sharding import PartitionSpec as P

ITERS = 3
HIGH = lax.Precision.HIGHEST


def partial_image(chosen, wtiles, vectors):
    blocks, count, tile, rank = chosen.shape
    shaped = vectors.reshape(blocks, tile, rank)
    scores = jnp.einsum("bkjr,bur->bkuj", chosen, shaped, precision=HIGH)
    back = jnp.einsum("bkuj,bkjr->bur", scores * wtiles, chosen, precision=HIGH)
    return back.reshape(blocks * tile, rank)


def local_terms(vectors, gram):
    return (
        jnp.dot(vectors, gram, preferred_element_type=jnp.float32, precision=HIGH) + 1.0 * vectors
    )


def update(state, image):
    solved, resid, direction, norm_now = state
    alpha = norm_now / (jnp.sum(direction * image, axis=1, keepdims=True) + 1e-06)
    solved = solved + alpha * direction
    resid = resid - alpha * image
    norm_next = jnp.sum(resid * resid, axis=1, keepdims=True)
    direction = resid + norm_next / (norm_now + 1e-06) * direction
    return (solved, resid, direction, norm_next)


def local(item_factors, weights, tile_ids, start_factors):
    slab = item_factors[0]
    rank = slab.shape[1]
    tile = weights.shape[2]
    gram = lax.psum(
        jnp.dot(slab.T, slab, preferred_element_type=jnp.float32, precision=HIGH), ("user", "item")
    )
    block = lax.all_gather(slab, "user", axis=0, tiled=True)
    vtiles = block.reshape(-1, tile, rank)
    chosen = jnp.take(vtiles, tile_ids[:, 0, :], axis=0)
    blocks = chosen.shape[0]
    prefs = jnp.where(weights > 0, 1.0 + weights, 0.0)
    rhs_part = jnp.einsum("bkuj,bkjr->bur", prefs, chosen, precision=HIGH).reshape(
        blocks * tile, rank
    )
    start_part = partial_image(chosen, weights, start_factors)
    rhs, image = lax.psum((rhs_part, start_part), "item")
    resid = rhs - image - local_terms(start_factors, gram)
    norm_now = jnp.sum(resid * resid, axis=1, keepdims=True)
    state = (start_factors, resid, resid, norm_now)
    for step in range(ITERS):
        direction = state[2]
        image = lax.psum(partial_image(chosen, weights, direction), "item")
        state = update(state, image + local_terms(direction, gram))
    return state[0]


def solution(mesh):
    in_specs = (
        P("item", "user", None),
        P("user", "item", None, None),
        P("user", "item", None),
        P("user", None),
    )
    out_specs = P("user", None)
    return jax.shard_map(local, mesh=mesh, in_specs=in_specs, out_specs=out_specs, check_vma=False)
```

profile of v0, /device:TPU:2, one launch (start us, length us, event | category | flops | bytes accessed | tf_op | source)
XLA Modules:
  0.0 901.7 jit_solution(9021807846128946891)
XLA Ops:
  7.4 0.7 all-gather.3.cloned.1.call-update
  8.1 0.0 all-reduce.7.cloned.1.call-start
  8.1 2.0 fusion.48
  10.1 0.0 all-reduce.7.cloned.1.call-update
  10.2 0.0 all-reduce.15.cloned.1.call-start
  10.2 0.7 compare_and_fusion
  10.9 0.7 compare_select_fusion
  11.6 0.1 reshape.116
  11.7 55.4 %all-gather.3.cloned.1.call-done = f32[1,4096,128]{2,1,0:T(8,128)} async-done(((f32[1,256,128]{2,1,0:T(8,128)}), f32[1,4096,128]{2,1,0:T(8,128)}) %all-gather.3.cloned.1.call-update) | async-done | bytes 2097168 | tf_op jit(solution)/shard_map/all_gather | solution.py:41
  67.0 6.0 gather_fusion
  73.0 11.9 %fusion.18 = f32[8,16,128,128]{2,3,1,0:T(8,128)S(1)} fusion(f32[8,128,128,1]{2,1,3,0:T(8,128)S(1)} %bitcast.77, f32[8,16,128,128]{3,2,1,0:T(8,128)} %bitcast.67, pred[8,16]{1,0:T(8,128)(4,1)S(1)} %compare_and_fusion), kind=kOutput, calls=%fused_computation.23 | convolution fusion | flops 3223322624 | bytes 17301632 | tf_op jit(solution)/shard_map/bkjr,bur->bkuj/dot_general | solution.py:13
  84.9 11.5 %fusion.3 = f32[8,128,128,1]{2,1,3,0:T(8,128)S(1)} fusion(f32[8,16,128,128]{3,2,1,0:T(8,128)} %param.5, f32[8,16,128,128]{2,3,1,0:T(8,128)S(1)} %fusion.18, f32[8,16,128,128]{3,2,1,0:T(8,128)S(1)} %bitcast.74, pred[8,16]{1,0:T(8,128)(4,1)S(1)} %compare_and_fusion), kind=kOutput, calls=%fused_computation.8 | convolution fusion | flops 3225419776 | bytes 25690240 | tf_op jit(solution)/shard_map/bkuj,bkjr->bur/dot_general | solution.py:14
  96.4 12.2 %fusion.4 = f32[8,128,128,1]{2,1,3,0:T(8,128)S(1)} fusion(f32[8,16,128,128]{3,2,1,0:T(8,128)} %param.5, f32[8,16,128,128]{3,2,1,0:T(8,128)S(1)} %bitcast.75, pred[8,16]{1,0:T(8,128)(4,1)S(1)} %compare_and_fusion), kind=kOutput, calls=%fused_computation.9 | convolution fusion | flops 3229614080 | bytes 17301632 | tf_op jit(solution)/shard_map/bkuj,bkjr->bur/dot_general | solution.py:46
  108.6 1.0 copy.5
  109.6 1.0 copy.6
  110.6 0.0 all-reduce.15.cloned.1.call-update
  110.6 0.0 all-reduce.9.cloned.1.call-start
  110.7 0.2 copy.10
  110.9 147.4 %all-reduce.7.cloned.1.call-done = f32[128,128]{1,0:T(8,128)} async-done(((f32[128,128]{1,0:T(8,128)}), f32[128,128]{1,0:T(8,128)}) %all-reduce.7.cloned.1.call-update) | async-done | bytes 65552 | tf_op jit(solution)/shard_map/psum | solution.py:38
  258.2 139.7 %all-reduce.15.cloned.1.call-done = (f32[1024,128]{0,1:T(8,128)}, f32[1024,128]{0,1:T(8,128)}) async-done(((f32[1024,128]{0,1:T(8,128)}, f32[1024,128]{0,1:T(8,128)}), (f32[1024,128]{0,1:T(8,128)}, f32[1024,128]{0,1:T(8,128)})) %all-reduce.15.cloned.1.call-update) | async-done | bytes 1048592 | tf_op jit(solution)/shard_map/psum | solution.py:50
  397.9 1.9 fusion.42
  399.9 0.2 copy.26
  400.1 10.3 %fusion.15 = f32[8,128,16,128]{3,1,2,0:T(8,128)S(1)} fusion(f32[8,128,128,1]{2,1,3,0:T(8,128)S(1)} %bitcast.83, f32[8,16,128,128]{3,2,1,0:T(8,128)} %bitcast.68, pred[8,16]{1,0:T(8,128)(4,1)S(1)} %compare_and_fusion), kind=kOutput, calls=%fused_computation.20 | convolution fusion | flops 3223322624 | bytes 17301632 | tf_op jit(solution)/shard_map/bkjr,bur->bkuj/dot_general | solution.py:13
  410.4 12.8 %fusion.2 = f32[8,128,128,1]{2,1,3,0:T(8,128)S(1)} fusion(f32[8,16,128,128]{3,2,1,0:T(8,128)} %param.5, f32[8,128,16,128]{3,1,2,0:T(8,128)S(1)} %fusion.15, f32[8,16,128,128]{3,2,1,0:T(8,128)} %bitcast.69, pred[8,16]{1,0:T(8,128)(4,1)S(1)} %compare_and_fusion), kind=kOutput, calls=%fused_computation.6 | convolution fusion | flops 3225419776 | bytes 25690240 | tf_op jit(solution)/shard_map/bkuj,bkjr->bur/dot_general | solution.py:14
  423.2 1.0 copy.27
  424.2 0.0 all-reduce.9.cloned.1.call-update
  424.2 0.0 all-reduce.11.cloned.1.call-start
  424.3 138.1 %all-reduce.9.cloned.1.call-done = f32[1024,128]{0,1:T(8,128)} async-done(((f32[1024,128]{0,1:T(8,128)}), f32[1024,128]{0,1:T(8,128)}) %all-reduce.9.cloned.1.call-update) | async-done | bytes 524304 | tf_op jit(solution)/shard_map/psum | solution.py:56
  562.4 1.7 multiply_reduce_fusion.3
  564.1 0.1 multiply_reduce_fusion.2
  564.2 0.1 multiply_add_fusion.2
  564.3 0.2 copy.28
  564.5 10.4 %fusion.12 = f32[8,128,16,128]{3,1,2,0:T(8,128)S(1)} fusion(f32[8,128,128,1]{2,1,3,0:T(8,128)S(1)} %bitcast.84, f32[8,16,128,128]{3,2,1,0:T(8,128)} %bitcast.70, pred[8,16]{1,0:T(8,128)(4,1)S(1)} %compare_and_fusion), kind=kOutput, calls=%fused_computation.17 | convolution fusion | flops 3223322624 | bytes 17301632 | tf_op jit(solution)/shard_map/bkjr,bur->bkuj/dot_general | solution.py:13
  574.9 12.7 %fusion.1 = f32[8,128,128,1]{2,1,3,0:T(8,128)S(1)} fusion(f32[8,16,128,128]{3,2,1,0:T(8,128)} %param.5, f32[8,128,16,128]{3,1,2,0:T(8,128)S(1)} %fusion.12, f32[8,16,128,128]{3,2,1,0:T(8,128)} %bitcast.71, pred[8,16]{1,0:T(8,128)(4,1)S(1)} %compare_and_fusion), kind=kOutput, calls=%fused_computation.4 | convolution fusion | flops 3225419776 | bytes 25690240 | tf_op jit(solution)/shard_map/bkuj,bkjr->bur/dot_general | solution.py:14
  587.6 1.0 copy.29
  588.7 0.0 all-reduce.13.cloned.1.call-start
  588.7 137.8 %all-reduce.11.cloned.1.call-done = f32[1024,128]{0,1:T(8,128)} async-done(((f32[1024,128]{0,1:T(8,128)}), f32[1024,128]{0,1:T(8,128)}) %all-reduce.11.cloned.1.call-update) | async-done | bytes 524304 | tf_op jit(solution)/shard_map/psum | solution.py:56
  726.5 1.7 multiply_reduce_fusion.1
  728.2 0.1 multiply_reduce_fusion
  728.3 0.1 multiply_add_fusion.1
  728.5 0.2 copy.30
  728.7 10.4 %fusion.9 = f32[8,128,16,128]{3,1,2,0:T(8,128)S(1)} fusion(f32[8,128,128,1]{2,1,3,0:T(8,128)S(1)} %bitcast.85, f32[8,16,128,128]{3,2,1,0:T(8,128)} %bitcast.72, pred[8,16]{1,0:T(8,128)(4,1)S(1)} %compare_and_fusion), kind=kOutput, calls=%fused_computation.14 | convolution fusion | flops 3223322624 | bytes 17301632 | tf_op jit(solution)/shard_map/bkjr,bur->bkuj/dot_general | solution.py:13
  739.1 12.7 %fusion = f32[8,128,128,1]{2,1,3,0:T(8,128)S(1)} fusion(f32[8,16,128,128]{3,2,1,0:T(8,128)} %param.5, f32[8,128,16,128]{3,1,2,0:T(8,128)S(1)} %fusion.9, f32[8,16,128,128]{3,2,1,0:T(8,128)} %bitcast.73, pred[8,16]{1,0:T(8,128)(4,1)S(1)} %compare_and_fusion), kind=kOutput, calls=%fused_computation.2 | convolution fusion | flops 3225419776 | bytes 25690240 | tf_op jit(solution)/shard_map/bkuj,bkjr->bur/dot_general | solution.py:14
  751.9 1.0 copy.31
  752.9 137.9 %all-reduce.13.cloned.1.call-done = f32[1024,128]{0,1:T(8,128)} async-done(((f32[1024,128]{0,1:T(8,128)}), f32[1024,128]{0,1:T(8,128)}) %all-reduce.13.cloned.1.call-update) | async-done | bytes 524304 | tf_op jit(solution)/shard_map/psum | solution.py:56
  890.7 1.7 fusion.47
  892.4 0.2 multiply_add_fusion
  892.6 1.0 copy.14
  (15 shorter events, 0.1 us)
Async XLA Ops:
  7.4 59.7 %all-gather.3.cloned.1.call-start = ((), (), s32[]{:S(2)}) async-start(), calls=%async_computation.4 | async-start | bytes 2228224 | tf_op jit(solution)/shard_map/all_gather | solution.py:41
  8.1 250.1 %all-reduce.7.cloned.1.call-start = ((), (), s32[]{:S(2)}) async-start(), calls=%async_computation | async-start | bytes 131072 | tf_op jit(solution)/shard_map/psum | solution.py:38
  10.2 387.8 %all-reduce.15.cloned.1.call-start = ((), (), s32[]{:S(2)}) async-start(), calls=%async_computation.5 | async-start | bytes 2097152 | tf_op jit(solution)/shard_map/psum | solution.py:50
  67.0 6.0 copy-start.1
  73.0 11.9 %copy-start = (f32[128,128,128]{2,1,0:T(8,128)S(1)}, f32[128,128,128]{2,1,0:T(8,128)}, u32[]{:S(2)}) copy-start(f32[128,128,128]{2,1,0:T(8,128)} %gather_fusion) | copy-start | bytes 25165828
  110.6 451.8 %all-reduce.9.cloned.1.call-start = ((), (), s32[]{:S(2)}) async-start(), calls=%async_computation.1 | async-start | bytes 1048576 | tf_op jit(solution)/shard_map/psum | solution.py:56
  410.4 151.9 %copy-start.2 = (f32[128,128]{1,0:T(8,128)S(1)}, f32[128,128]{1,0:T(8,128)}, u32[]{:S(2)}) copy-start(f32[128,128]{1,0:T(8,128)} %all-reduce.7.cloned.1.call-done) | copy-start | bytes 196612
  424.2 302.3 %all-reduce.11.cloned.1.call-start = ((), (), s32[]{:S(2)}) async-start(), calls=%async_computation.2 | async-start | bytes 1048576 | tf_op jit(solution)/shard_map/psum | solution.py:56
  588.7 302.1 %all-reduce.13.cloned.1.call-start = ((), (), s32[]{:S(2)}) async-start(), calls=%async_computation.3 | async-start | bytes 1048576 | tf_op jit(solution)/shard_map/psum | solution.py:56
Sparse Core Ops, SparseCore 0:
  10.8 56.1 all-gather.2
Sparse Core Ops, SparseCore 1:
  14.1 244.1 all-reduce.6
  260.8 137.1 all-reduce.14
  424.3 138.0 all-reduce.8
  588.7 137.7 all-reduce.10
  753.0 137.7 all-reduce.12
where the time goes:
time: 909 us; the launch traced here: 902 us
  waiting for transfers between devices  757 us (83%)
  matrix products  114 us (13%)
  between operations  15.7 us (2%)
  local copies, waits for them, and re-layouts  12.8 us (1%)
    psum x3, waiting for transfers between devices, local(): image = lax.psum(partial_image(chosen, weights, direction), 'item')  414 us
    psum x1, waiting for transfers between devices, local(): lax.psum(jnp.dot(slab.T, slab, preferred_element_type=jnp.float32, precis...  147 us
    psum x1, waiting for transfers between devices, local(): rhs, image = lax.psum((rhs_part, start_part), 'item')  140 us
    all_gather x1, waiting for transfers between devices, local(): block = lax.all_gather(slab, 'user', axis=0, tiled=True)  55.4 us
    dot_general x4, matrix products, partial_image(): back = jnp.einsum('bkuj,bkjr->bur', scores * wtiles, chosen, precision=HIGH)  49.7 us
    dot_general x4, matrix products, partial_image(): scores = jnp.einsum('bkjr,bur->bkuj', chosen, shaped, precision=HIGH)  43 us
  transfers between devices with their start and end apart: 6, of which 6 were waited for; matrix products, arithmetic and copies ran while one was open for 5% of the time, Pallas kernels for 0%

commit v1 on v0

--- a/solution.py
+++ b/solution.py
@@ -36,7 +36,8 @@
     rank = slab.shape[1]
     tile = weights.shape[2]
     gram = lax.psum(
-        jnp.dot(slab.T, slab, preferred_element_type=jnp.float32, precision=HIGH), ("user", "item")
+        lax.psum(jnp.dot(slab.T, slab, preferred_element_type=jnp.float32, precision=HIGH), "user"),
+        "item",
     )
     block = lax.all_gather(slab, "user", axis=0, tiled=True)
     vtiles = block.reshape(-1, tile, rank)

time: 909 us -> 855 us (0.941)
  waiting for transfers between devices: 757 us -> 704 us
    psum x1, waiting for transfers between devices: 147 us -> 89.3 us  [local(): lax.psum(jnp.dot(slab.T, slab, preferred_element_type=jnp.float32, precis...]
  transfers between devices with their start and end apart: 6 -> 6, of which waited for: 6 -> 6; matrix products, arithmetic and copies ran while one was open for 5% -> 6% of each run, Pallas kernels for 0% -> 0%
where the time goes in v1:
time: 855 us; the launch traced here: 847 us
  waiting for transfers between devices  704 us (82%)
  matrix products  114 us (13%)
  between operations  13.9 us (2%)
  local copies, waits for them, and re-layouts  12.8 us (1%)
    psum x3, waiting for transfers between devices, local(): image = lax.psum(partial_image(chosen, weights, direction), 'item')  414 us
    psum x1, waiting for transfers between devices, local(): lax.psum(lax.psum(jnp.dot(slab.T, slab, preferred_element_type=jnp.float3...  145 us
    psum x1, waiting for transfers between devices, local(): lax.psum(jnp.dot(slab.T, slab, preferred_element_type=jnp.float32, precis...  89.3 us
    all_gather x1, waiting for transfers between devices, local(): block = lax.all_gather(slab, 'user', axis=0, tiled=True)  55.3 us
    dot_general x4, matrix products, partial_image(): back = jnp.einsum('bkuj,bkjr->bur', scores * wtiles, chosen, precision=HIGH)  49.7 us
    dot_general x4, matrix products, partial_image(): scores = jnp.einsum('bkjr,bur->bkuj', chosen, shaped, precision=HIGH)  43.3 us
  transfers between devices with their start and end apart: 6, of which 6 were waited for; matrix products, arithmetic and copies ran while one was open for 6% of the time, Pallas kernels for 0%

profile of v1, /device:TPU:2, one launch (start us, length us, event | category | flops | bytes accessed | tf_op | source)
XLA Modules:
  0.0 847.2 jit_solution(9180157162079011603)
XLA Ops:
  6.5 0.7 all-gather.3.cloned.1.call-update
  7.3 0.0 all-reduce.7.cloned.1.call-start
  7.3 2.0 fusion.48
  9.3 0.0 all-reduce.7.cloned.1.call-update
  9.3 0.0 all-reduce.15.cloned.1.call-start
  9.4 0.7 compare_and_fusion
  10.1 0.7 compare_select_fusion
  10.7 0.1 reshape.116
  10.8 55.3 %all-gather.3.cloned.1.call-done = f32[1,4096,128]{2,1,0:T(8,128)} async-done(((f32[1,256,128]{2,1,0:T(8,128)}), f32[1,4096,128]{2,1,0:T(8,128)}) %all-gather.3.cloned.1.call-update) | async-done | bytes 2097168 | tf_op jit(solution)/shard_map/all_gather | solution.py:42
  66.1 6.0 gather_fusion
  72.1 11.9 %fusion.18 = f32[8,16,128,128]{2,3,1,0:T(8,128)S(1)} fusion(f32[8,128,128,1]{2,1,3,0:T(8,128)S(1)} %bitcast.77, f32[8,16,128,128]{3,2,1,0:T(8,128)} %bitcast.67, pred[8,16]{1,0:T(8,128)(4,1)S(1)} %compare_and_fusion), kind=kOutput, calls=%fused_computation.23 | convolution fusion | flops 3223322624 | bytes 17301632 | tf_op jit(solution)/shard_map/bkjr,bur->bkuj/dot_general | solution.py:13
  84.0 11.5 %fusion.3 = f32[8,128,128,1]{2,1,3,0:T(8,128)S(1)} fusion(f32[8,16,128,128]{3,2,1,0:T(8,128)} %param.5, f32[8,16,128,128]{2,3,1,0:T(8,128)S(1)} %fusion.18, f32[8,16,128,128]{3,2,1,0:T(8,128)S(1)} %bitcast.74, pred[8,16]{1,0:T(8,128)(4,1)S(1)} %compare_and_fusion), kind=kOutput, calls=%fused_computation.8 | convolution fusion | flops 3225419776 | bytes 25690240 | tf_op jit(solution)/shard_map/bkuj,bkjr->bur/dot_general | solution.py:14
  95.5 12.0 %fusion.4 = f32[8,128,128,1]{2,1,3,0:T(8,128)S(1)} fusion(f32[8,16,128,128]{3,2,1,0:T(8,128)} %param.5, f32[8,16,128,128]{3,2,1,0:T(8,128)S(1)} %bitcast.75, pred[8,16]{1,0:T(8,128)(4,1)S(1)} %compare_and_fusion), kind=kOutput, calls=%fused_computation.9 | convolution fusion | flops 3229614080 | bytes 17301632 | tf_op jit(solution)/shard_map/bkuj,bkjr->bur/dot_general | solution.py:47
  107.5 1.0 copy.5
  108.5 1.0 copy.6
  109.5 89.3 %all-reduce.7.cloned.1.call-done = f32[128,128]{1,0:T(8,128)} async-done(((f32[128,128]{1,0:T(8,128)}), f32[128,128]{1,0:T(8,128)}) %all-reduce.7.cloned.1.call-update) | async-done | bytes 65552 | tf_op jit(solution)/shard_map/psum | solution.py:39
  198.9 0.0 all-reduce.9.cloned.1.call-start
  198.9 0.2 copy.10
  199.1 144.8 %all-reduce.15.cloned.1.call-done = (f32[128,128]{1,0:T(8,128)}, f32[1024,128]{0,1:T(8,128)}, f32[1024,128]{0,1:T(8,128)}) async-done(((f32[128,128]{1,0:T(8,128)}, f32[1024,128]{0,1:T(8,128)}, f32[1024,128]{0,1:T(8,128)}), (f32[128,128]{1,0:T(8,128)}, f32[1024,128]{0,1:T(8,128)}, f32[1024,128]{0,1:T(8,128)})) %all-reduce.15.cloned.1.call-update) | async-done | bytes 1114128 | tf_op jit(solution)/shard_map/psum | solution.py:38
  343.9 1.9 fusion.42
  345.8 0.2 copy.26
  346.0 10.7 %fusion.15 = f32[8,128,16,128]{3,1,2,0:T(8,128)S(1)} fusion(f32[8,128,128,1]{2,1,3,0:T(8,128)S(1)} %bitcast.83, f32[8,16,128,128]{3,2,1,0:T(8,128)} %bitcast.68, pred[8,16]{1,0:T(8,128)(4,1)S(1)} %compare_and_fusion), kind=kOutput, calls=%fused_computation.20 | convolution fusion | flops 3223322624 | bytes 17301632 | tf_op jit(solution)/shard_map/bkjr,bur->bkuj/dot_general | solution.py:13
  356.8 12.8 %fusion.2 = f32[8,128,128,1]{2,1,3,0:T(8,128)S(1)} fusion(f32[8,16,128,128]{3,2,1,0:T(8,128)} %param.5, f32[8,128,16,128]{3,1,2,0:T(8,128)S(1)} %fusion.15, f32[8,16,128,128]{3,2,1,0:T(8,128)} %bitcast.69, pred[8,16]{1,0:T(8,128)(4,1)S(1)} %compare_and_fusion), kind=kOutput, calls=%fused_computation.6 | convolution fusion | flops 3225419776 | bytes 25690240 | tf_op jit(solution)/shard_map/bkuj,bkjr->bur/dot_general | solution.py:14
  369.5 1.0 copy.27
  370.5 0.0 all-reduce.9.cloned.1.call-update
  370.6 0.0 all-reduce.11.cloned.1.call-start
  370.6 137.8 %all-reduce.9.cloned.1.call-done = f32[1024,128]{0,1:T(8,128)} async-done(((f32[1024,128]{0,1:T(8,128)}), f32[1024,128]{0,1:T(8,128)}) %all-reduce.9.cloned.1.call-update) | async-done | bytes 524304 | tf_op jit(solution)/shard_map/psum | solution.py:57
  508.4 1.7 multiply_reduce_fusion.3
  510.2 0.1 multiply_reduce_fusion.2
  510.3 0.1 multiply_add_fusion.2
  510.3 0.2 copy.28
  510.5 10.3 %fusion.12 = f32[8,128,16,128]{3,1,2,0:T(8,128)S(1)} fusion(f32[8,128,128,1]{2,1,3,0:T(8,128)S(1)} %bitcast.84, f32[8,16,128,128]{3,2,1,0:T(8,128)} %bitcast.70, pred[8,16]{1,0:T(8,128)(4,1)S(1)} %compare_and_fusion), kind=kOutput, calls=%fused_computation.17 | convolution fusion | flops 3223322624 | bytes 17301632 | tf_op jit(solution)/shard_map/bkjr,bur->bkuj/dot_general | solution.py:13
  520.9 12.7 %fusion.1 = f32[8,128,128,1]{2,1,3,0:T(8,128)S(1)} fusion(f32[8,16,128,128]{3,2,1,0:T(8,128)} %param.5, f32[8,128,16,128]{3,1,2,0:T(8,128)S(1)} %fusion.12, f32[8,16,128,128]{3,2,1,0:T(8,128)} %bitcast.71, pred[8,16]{1,0:T(8,128)(4,1)S(1)} %compare_and_fusion), kind=kOutput, calls=%fused_computation.4 | convolution fusion | flops 3225419776 | bytes 25690240 | tf_op jit(solution)/shard_map/bkuj,bkjr->bur/dot_general | solution.py:14
  533.6 1.0 copy.29
  534.6 0.0 all-reduce.11.cloned.1.call-update
  534.7 0.0 all-reduce.13.cloned.1.call-start
  534.7 138.2 %all-reduce.11.cloned.1.call-done = f32[1024,128]{0,1:T(8,128)} async-done(((f32[1024,128]{0,1:T(8,128)}), f32[1024,128]{0,1:T(8,128)}) %all-reduce.11.cloned.1.call-update) | async-done | bytes 524304 | tf_op jit(solution)/shard_map/psum | solution.py:57
  672.9 1.7 multiply_reduce_fusion.1
  674.6 0.1 multiply_reduce_fusion
  674.7 0.1 multiply_add_fusion.1
  674.9 0.2 copy.30
  675.1 10.4 %fusion.9 = f32[8,128,16,128]{3,1,2,0:T(8,128)S(1)} fusion(f32[8,128,128,1]{2,1,3,0:T(8,128)S(1)} %bitcast.85, f32[8,16,128,128]{3,2,1,0:T(8,128)} %bitcast.72, pred[8,16]{1,0:T(8,128)(4,1)S(1)} %compare_and_fusion), kind=kOutput, calls=%fused_computation.14 | convolution fusion | flops 3223322624 | bytes 17301632 | tf_op jit(solution)/shard_map/bkjr,bur->bkuj/dot_general | solution.py:13
  685.4 12.7 %fusion = f32[8,128,128,1]{2,1,3,0:T(8,128)S(1)} fusion(f32[8,16,128,128]{3,2,1,0:T(8,128)} %param.5, f32[8,128,16,128]{3,1,2,0:T(8,128)S(1)} %fusion.9, f32[8,16,128,128]{3,2,1,0:T(8,128)} %bitcast.73, pred[8,16]{1,0:T(8,128)(4,1)S(1)} %compare_and_fusion), kind=kOutput, calls=%fused_computation.2 | convolution fusion | flops 3225419776 | bytes 25690240 | tf_op jit(solution)/shard_map/bkuj,bkjr->bur/dot_general | solution.py:14
  698.2 1.0 copy.31
  699.2 138.0 %all-reduce.13.cloned.1.call-done = f32[1024,128]{0,1:T(8,128)} async-done(((f32[1024,128]{0,1:T(8,128)}), f32[1024,128]{0,1:T(8,128)}) %all-reduce.13.cloned.1.call-update) | async-done | bytes 524304 | tf_op jit(solution)/shard_map/psum | solution.py:57
  837.2 1.7 fusion.47
  838.9 0.2 multiply_add_fusion
  839.1 1.0 copy.14
  (15 shorter events, 0.1 us)
Async XLA Ops:
  6.5 59.6 %all-gather.3.cloned.1.call-start = ((), (), s32[]{:S(2)}) async-start(), calls=%async_computation.4 | async-start | bytes 2228224 | tf_op jit(solution)/shard_map/all_gather | solution.py:42
  7.3 191.6 %all-reduce.7.cloned.1.call-start = ((), (), s32[]{:S(2)}) async-start(), calls=%async_computation | async-start | bytes 131072 | tf_op jit(solution)/shard_map/psum | solution.py:39
  9.3 334.6 %all-reduce.15.cloned.1.call-start = ((), (), s32[]{:S(2)}) async-start(), calls=%async_computation.5 | async-start | bytes 2228224 | tf_op jit(solution)/shard_map/psum | solution.py:38
  66.1 6.0 copy-start.1
  72.1 11.9 %copy-start = (f32[128,128,128]{2,1,0:T(8,128)S(1)}, f32[128,128,128]{2,1,0:T(8,128)}, u32[]{:S(2)}) copy-start(f32[128,128,128]{2,1,0:T(8,128)} %gather_fusion) | copy-start | bytes 25165828
  198.9 309.5 %all-reduce.9.cloned.1.call-start = ((), (), s32[]{:S(2)}) async-start(), calls=%async_computation.1 | async-start | bytes 1048576 | tf_op jit(solution)/shard_map/psum | solution.py:57
  356.7 151.7 %copy-start.2 = (f32[128,128]{1,0:T(8,128)S(1)}, f32[128,128]{1,0:T(8,128)}, u32[]{:S(2)}) copy-start(f32[128,128]{1,0:T(8,128)} %get-tuple-element.7) | copy-start | bytes 196612
  370.6 302.3 %all-reduce.11.cloned.1.call-start = ((), (), s32[]{:S(2)}) async-start(), calls=%async_computation.2 | async-start | bytes 1048576 | tf_op jit(solution)/shard_map/psum | solution.py:57
  534.7 302.5 %all-reduce.13.cloned.1.call-start = ((), (), s32[]{:S(2)}) async-start(), calls=%async_computation.3 | async-start | bytes 1048576 | tf_op jit(solution)/shard_map/psum | solution.py:57
Sparse Core Ops, SparseCore 0:
  10.0 56.0 all-gather.2
  68.7 130.0 all-reduce.6
  201.7 142.1 all-reduce.14
  370.7 137.6 all-reduce.8
  534.8 138.0 all-reduce.10
  699.3 137.8 all-reduce.12
